TPU v7x, 32 devices: a whole 2x2x4 slice. The times are simulated.
32 devices in a mesh: elec: 4 (over y, core), pix: 8 (over z, x).
Axes of the slice: x: 2, y: 2, z: 4, core: 2. Of those that a mesh axis runs over, the one named last changes fastest.
Arguments:
- wavefronts: bfloat16 [1536, 2, 320, 256], P('elec', None, 'pix'), may hold values from -40 to 40, as said below
- trial_modes: float32 [2, 32, 320, 256], P(None, None, 'pix'), may hold values from -6 to 6
Outputs:
- sample_modes: float32 [2, 32, 320, 256], P(None, 'elec', None, 'pix')
Inputs may be any that keep to these rules, and one draw needn't show every extreme that they name: `wavefronts`: field samples of each electron's wavefront.
All inputs are finite; a program needn't handle non-finite values.
Results may differ from a plain program's by a relative error of at most 0.0075.
Values may be sent and summed in bfloat16 or wider, within the bound.
A program may use at most 128 MiB of HBM per device.

v0:
```python
import math
import jax
import jax.numpy as jnp
from jax import lax
from jax.sharding import PartitionSpec as P

ITERS = 2
NS_STEPS = 8
HIGH = lax.Precision.HIGHEST


def project(wave_re, wave_im, modes_low):
    stacked = modes_low.reshape(-1, modes_low.shape[2])
    swapped = jnp.concatenate([-modes_low[1], modes_low[0]], axis=0)
    contract = (((1,), (1,)), ((), ()))
    real_side = lax.dot_general(wave_re, stacked, contract, preferred_element_type=jnp.float32)
    imag_side = lax.dot_general(wave_im, swapped, contract, preferred_element_type=jnp.float32)
    return real_side + imag_side


def covariance(waves, projected, mode_count):
    pixels = waves.shape[1] // 2
    width = projected.shape[1]
    upper = projected.astype(jnp.bfloat16)
    lower = (projected - upper.astype(jnp.float32)).astype(jnp.bfloat16)
    both = jnp.concatenate([upper, lower], axis=1)
    stacked = lax.dot_general(
        both, waves, (((0,), (0,)), ((), ())), preferred_element_type=jnp.float32
    )
    blocks = stacked[:width] + stacked[width:]
    real_part = blocks[:mode_count, :pixels] + blocks[mode_count:, pixels:]
    imag_part = blocks[mode_count:, :pixels] - blocks[:mode_count, pixels:]
    return jnp.stack([real_part, imag_part])


def gram_matrix(fields):
    flat = fields.reshape(-1, fields.shape[2])
    return jnp.dot(flat, flat.T, precision=HIGH)


def lowdin(gram_raw, mode_count):
    gram_re = gram_raw[:mode_count, :mode_count] + gram_raw[mode_count:, mode_count:]
    gram_im = gram_raw[:mode_count, mode_count:] - gram_raw[mode_count:, :mode_count]
    embedded = jnp.concatenate(
        [jnp.concatenate([gram_re, -gram_im], 1), jnp.concatenate([gram_im, gram_re], 1)], 0
    )
    trace_value = jnp.trace(embedded)
    scaled = embedded / trace_value
    identity = jnp.eye(2 * mode_count, dtype=embedded.dtype)
    inverse_root = identity
    for iteration in range(NS_STEPS):
        correction = 1.5 * identity - 0.5 * jnp.dot(inverse_root, scaled, precision=HIGH)
        scaled = jnp.dot(scaled, correction, precision=HIGH)
        inverse_root = jnp.dot(correction, inverse_root, precision=HIGH)
    return (inverse_root / jnp.sqrt(trace_value)).T


def rotate(rotation, fields):
    flat = fields.reshape(-1, fields.shape[2])
    return jnp.dot(rotation, flat, precision=HIGH).reshape(fields.shape)


def dft_table(length):
    index = jnp.arange(length, dtype=jnp.int32)
    product = index[:, None] * index[None, :] % length
    angle = 2.0 * math.pi / length * product.astype(jnp.float32)
    return (jnp.cos(angle), -jnp.sin(angle))


def chirp_phase(row_pos, col_pos, row_total, col_total, factor):
    row_term = (row_pos - row_total / 2.0) ** 2 / row_total
    col_term = (col_pos - col_total / 2.0) ** 2 / col_total
    angle = math.pi * factor * (row_term[:, None] + col_term[None, :])
    return (jnp.cos(angle), jnp.sin(angle))


def column_section(field, row_pos, row_total, col_total):
    col_pos = jnp.arange(col_total, dtype=jnp.float32)
    chirp_re, chirp_im = chirp_phase(row_pos, col_pos, row_total, col_total, 0.5)
    launch_re = chirp_re * field[0] - chirp_im * field[1]
    launch_im = chirp_re * field[1] + chirp_im * field[0]
    table_re, table_im = dft_table(col_total)
    spec_re = jnp.einsum("mry,yv->mrv", launch_re, table_re, precision=HIGH) - jnp.einsum(
        "mry,yv->mrv", launch_im, table_im, precision=HIGH
    )
    spec_im = jnp.einsum("mry,yv->mrv", launch_re, table_im, precision=HIGH) + jnp.einsum(
        "mry,yv->mrv", launch_im, table_re, precision=HIGH
    )
    return jnp.stack([spec_re, spec_im])


def row_section(spectrum, col_pos, row_total, col_total):
    table_re, table_im = dft_table(row_total)
    out_re = jnp.einsum("ux,mxv->muv", table_re, spectrum[0], precision=HIGH) - jnp.einsum(
        "ux,mxv->muv", table_im, spectrum[1], precision=HIGH
    )
    out_im = jnp.einsum("ux,mxv->muv", table_re, spectrum[1], precision=HIGH) + jnp.einsum(
        "ux,mxv->muv", table_im, spectrum[0], precision=HIGH
    )
    row_pos = jnp.arange(row_total, dtype=jnp.float32)
    chirp_re, chirp_im = chirp_phase(row_pos, col_pos, row_total, col_total, 0.25)
    return jnp.stack([chirp_re * out_re - chirp_im * out_im, chirp_re * out_im + chirp_im * out_re])


def pixel_sum(partial_value):
    return lax.psum(partial_value, "pix")


def shards(wavefronts, trial_modes):
    electrons_dev, _, rows_dev, cols = wavefronts.shape
    mode_count = trial_modes.shape[1]
    pixels = rows_dev * cols
    groups = lax.axis_size("elec")
    mode_share = mode_count // groups
    waves = wavefronts.reshape(electrons_dev, 2 * pixels)
    wave_re = waves[:, :pixels]
    wave_im = waves[:, pixels:]
    modes = trial_modes.reshape(2, mode_count, pixels)
    projected_part = project(wave_re, wave_im, modes.astype(jnp.bfloat16))
    share_low = None
    share_modes = None
    for iteration in range(ITERS):
        if iteration > 0:
            projected_part = project(
                wave_re, wave_im, lax.all_gather(share_low, "elec", axis=2, tiled=True)
            )
        projected = pixel_sum(projected_part)
        applied_share = lax.psum_scatter(
            covariance(waves, projected, mode_count), "elec", scatter_dimension=2, tiled=True
        )
        gram_total = lax.psum(gram_matrix(applied_share), ("elec", "pix"))
        share_modes = rotate(lowdin(gram_total, mode_count), applied_share)
        share_low = share_modes.astype(jnp.bfloat16)
    local_modes = lax.all_to_all(share_modes, "elec", split_axis=1, concat_axis=2, tiled=True)
    field = local_modes.reshape(2, mode_share, rows_dev, cols)
    pix_count = lax.axis_size("pix")
    row_total = rows_dev * pix_count
    row_pos = (lax.axis_index("pix") * rows_dev + jnp.arange(rows_dev, dtype=jnp.int32)).astype(
        jnp.float32
    )
    spectrum = column_section(field, row_pos, row_total, cols)
    column_block = lax.all_to_all(spectrum, "pix", split_axis=3, concat_axis=2, tiled=True)
    col_width = column_block.shape[3]
    col_pos = (lax.axis_index("pix") * col_width + jnp.arange(col_width, dtype=jnp.int32)).astype(
        jnp.float32
    )
    return row_section(column_block, col_pos, row_total, cols)


def solution(mesh):
    in_specs = (P("elec", None, "pix", None), P(None, None, "pix", None))
    out_specs = P(None, "elec", None, "pix")
    return jax.shard_map(shards, mesh=mesh, in_specs=in_specs, out_specs=out_specs, check_vma=False)
```

profile of v0, /device:TPU:0, one launch (start us, length us, event | category | flops | bytes accessed | tf_op | source)
XLA Modules:
  0.0 470.5 jit_solution(15132005642279305516)
XLA Ops:
  6.5 11.1 %copy.19 = bf16[48,8,80,256]{3,1,2,0:T(8,128)(2,1)S(1)} copy(bf16[48,8,80,256]{3,2,1,0:T(8,128)(2,1)} %bitcast.196) | data formatting | bytes 31457280
  18.4 2.5 fusion.6
  23.2 3.2 fusion.27
  26.4 73.0 %all-reduce.3.cloned.1.call-done = f32[384,64]{0,1:T(8,128)} async-done(((f32[384,64]{0,1:T(8,128)}), f32[384,64]{0,1:T(8,128)}) %all-reduce.3.cloned.1.call-update) | async-done | bytes 98320 | tf_op jit(solution)/shard_map/psum | solution.py:106
  100.4 7.0 %fusion.98 = f32[128,20480]{1,0:T(8,128)S(1)} fusion(bf16[384,20480]{1,0:T(8,128)(2,1)} %bitcast.192, bf16[384,64]{0,1:T(8,128)(2,1)S(1)} %get-tuple-element.11, bf16[384,64]{0,1:T(8,128)(2,1)S(1)} %get-tuple-element.12), kind=kOutput, calls=%fused_computation.123 | convolution fusion | flops 2013462528 | bytes 26312704 | tf_op jit(solution)/shard_map/dot_general | solution.py:27
  110.0 33.6 %reduce-scatter.3.cloned.1.call-done = f32[2,32,2560]{2,1,0:T(8,128)} async-done(((f32[2,32,10240]{2,1,0:T(8,128)}), f32[2,32,2560]{2,1,0:T(8,128)}) %reduce-scatter.3.cloned.1.call-update) | async-done | bytes 655376 | tf_op jit(solution)/shard_map/reduce_scatter | solution.py:128
  145.7 39.4 %psum.29 = f32[64,64]{1,0:T(8,128)S(1)} all-reduce(f32[64,64]{1,0:T(8,128)S(1)} %fusion.152), channel_id=1, replica_groups=mesh['elec'=4,'pix'=8] {'elec','pix'}, use_global_device_ids=true, to_apply=%region_2.0 | all-reduce | flops 4096 | bytes 32768 | tf_op jit(solution)/shard_map/psum | solution.py:131
  193.9 18.5 %all-gather.2.cloned.1.call-done = bf16[2,32,10240]{2,1,0:T(8,128)(2,1)} async-done(((bf16[2,32,2560]{2,1,0:T(8,128)(2,1)}), bf16[2,32,10240]{2,1,0:T(8,128)(2,1)}) %all-gather.2.cloned.1.call-update) | async-done | bytes 1310736 | tf_op jit(solution)/shard_map/all_gather | solution.py:125
  213.8 5.9 %fusion = f32[64,384]{1,0:T(8,128)S(1)} fusion(bf16[384,20480]{1,0:T(8,128)(2,1)} %bitcast.193, bf16[32,10240]{1,0:T(8,128)(2,1)S(1)} %get-tuple-element.20, bf16[32,10240]{1,0:T(8,128)(2,1)S(1)} %get-tuple-element.19), kind=kOutput, calls=%fused_computation | convolution fusion | flops 505937920 | bytes 9273344 | tf_op jit(solution)/shard_map/dot_general | solution.py:17
  219.7 6.4 %fusion.35 = f32[384,64]{0,1:T(8,128)} fusion(f32[64,384]{1,0:T(8,128)S(1)} %fusion, bf16[64,10240]{1,0:T(8,128)(2,1)S(1)} %bitcast.208, bf16[384,20480]{1,0:T(8,128)(2,1)} %bitcast.194), kind=kOutput, calls=%fused_computation.38 | convolution fusion | flops 503341056 | bytes 9371648 | tf_op jit(solution)/shard_map/dot_general | solution.py:16
  226.2 70.3 %all-reduce.5.cloned.1.call-done = f32[384,64]{0,1:T(8,128)} async-done(((f32[384,64]{0,1:T(8,128)}), f32[384,64]{0,1:T(8,128)}) %all-reduce.5.cloned.1.call-update) | async-done | bytes 98320 | tf_op jit(solution)/shard_map/psum | solution.py:106
  297.5 7.0 %fusion.102 = f32[128,20480]{1,0:T(8,128)S(1)} fusion(bf16[384,20480]{1,0:T(8,128)(2,1)} %bitcast.195, bf16[384,64]{0,1:T(8,128)(2,1)S(1)} %get-tuple-element.7, bf16[384,64]{0,1:T(8,128)(2,1)S(1)} %get-tuple-element.8), kind=kOutput, calls=%fused_computation.127 | convolution fusion | flops 2013462528 | bytes 26312704 | tf_op jit(solution)/shard_map/dot_general | solution.py:27
  307.0 33.7 %reduce-scatter.5.cloned.1.call-done = f32[2,32,2560]{2,1,0:T(8,128)} async-done(((f32[2,32,10240]{2,1,0:T(8,128)}), f32[2,32,2560]{2,1,0:T(8,128)}) %reduce-scatter.5.cloned.1.call-update) | async-done | bytes 655376 | tf_op jit(solution)/shard_map/reduce_scatter | solution.py:128
  342.8 39.4 %psum.31 = f32[64,64]{1,0:T(8,128)S(1)} all-reduce(f32[64,64]{1,0:T(8,128)S(1)} %fusion.165), channel_id=1, replica_groups=mesh['elec'=4,'pix'=8] {'elec','pix'}, use_global_device_ids=true, to_apply=%region_6.7 | all-reduce | flops 4096 | bytes 32768 | tf_op jit(solution)/shard_map/psum | solution.py:131
  391.1 3.7 all-to-all-start
  395.1 9.9 %all-to-all-done = f32[2,32,2560]{2,0,1:T(2,128)S(1)} async-done(((f32[2,32,2560]{2,0,1:T(2,128)}), f32[2,32,2560]{2,0,1:T(2,128)S(1)}, u32[]{:S(2)}, u32[]{:S(2)}) %all-to-all-start) | async-done | bytes 655392 | tf_op jit(solution)/shard_map/all_to_all | solution.py:134
  413.3 2.9 reshape.190
  416.2 5.2 %all-to-all-start.1 = ((f32[8,1,20480]{2,1,0:T(1,128)}), f32[8,1,20480]{2,1,0:T(1,128)S(1)}, u32[]{:S(2)}, u32[]{:S(2)}) async-start(f32[8,1,20480]{2,1,0:T(1,128)} %reshape.190), calls=%async_computation.3 | async-start | bytes 1310720 | tf_op jit(solution)/shard_map/all_to_all | solution.py:142
  421.7 16.7 %all-to-all-done.1 = f32[8,1,20480]{2,1,0:T(1,128)S(1)} async-done(((f32[8,1,20480]{2,1,0:T(1,128)}), f32[8,1,20480]{2,1,0:T(1,128)S(1)}, u32[]{:S(2)}, u32[]{:S(2)}) %all-to-all-start.1) | async-done | bytes 655392 | tf_op jit(solution)/shard_map/all_to_all | solution.py:142
  441.1 3.0 reshape.191
  450.5 2.8 fusion.59
  454.1 2.8 fusion.61
  456.9 2.8 fusion.18
  459.7 2.9 subtract_bitcast_fusion
  (117 shorter events, 50.8 us)
Async XLA Ops:
  6.5 92.9 %all-reduce.3.cloned.1.call-start = ((), (), s32[]{:S(2)}) async-start(), calls=%async_computation.4 | async-start | bytes 196608 | tf_op jit(solution)/shard_map/psum | solution.py:106
  6.5 11.1 %copy-start.4 = (f32[2,32,40,256]{3,2,1,0:T(8,128)S(1)}, f32[2,32,40,256]{3,2,1,0:T(8,128)}, u32[]{:S(2)}) copy-start(f32[2,32,40,256]{3,2,1,0:T(8,128)} %param.3) | copy-start | bytes 7864324
  17.7 5.5 %copy-start = (bf16[48,8,80,256]{3,1,2,0:T(8,128)(2,1)}, bf16[48,8,80,256]{3,1,2,0:T(8,128)(2,1)S(1)}, u32[]{:S(2)}) copy-start(bf16[48,8,80,256]{3,1,2,0:T(8,128)(2,1)S(1)} %copy.19) | copy-start | bytes 47185924
  26.4 117.3 %reduce-scatter.3.cloned.1.call-start = ((), (), s32[]{:S(2)}) async-start(), calls=%async_computation.5 | async-start | bytes 3276800 | tf_op jit(solution)/shard_map/reduce_scatter | solution.py:128
  110.0 102.5 %all-gather.2.cloned.1.call-start = ((), (), s32[]{:S(2)}) async-start(), calls=%async_computation.6 | async-start | bytes 1638400 | tf_op jit(solution)/shard_map/all_gather | solution.py:125
  143.7 48.3 %copy-start.2 = (f32[2,32,2560]{2,1,0:T(8,128)S(1)}, f32[2,32,2560]{2,1,0:T(8,128)}, u32[]{:S(2)}) copy-start(f32[2,32,2560]{2,1,0:T(8,128)} %reduce-scatter.3.cloned.1.call-done) | copy-start | bytes 1966084
  193.4 103.1 %all-reduce.5.cloned.1.call-start = ((), (), s32[]{:S(2)}) async-start(), calls=%async_computation.7 | async-start | bytes 196608 | tf_op jit(solution)/shard_map/psum | solution.py:106
  213.8 5.9 %copy-start.5 = (bf16[2,32,10240]{2,1,0:T(8,128)(2,1)S(1)}, bf16[2,32,10240]{2,1,0:T(8,128)(2,1)}, u32[]{:S(2)}) copy-start(bf16[2,32,10240]{2,1,0:T(8,128)(2,1)} %all-gather.2.cloned.1.call-done) | copy-start | bytes 3932164
  226.2 114.6 %reduce-scatter.5.cloned.1.call-start = ((), (), s32[]{:S(2)}) async-start(), calls=%async_computation.8 | async-start | bytes 3276800 | tf_op jit(solution)/shard_map/reduce_scatter | solution.py:128
  340.7 48.3 %copy-start.1 = (f32[2,32,2560]{2,1,0:T(8,128)S(1)}, f32[2,32,2560]{2,1,0:T(8,128)}, u32[]{:S(2)}) copy-start(f32[2,32,2560]{2,1,0:T(8,128)} %reduce-scatter.5.cloned.1.call-done) | copy-start | bytes 1966084
  391.1 13.9 %all-to-all-start = ((f32[2,32,2560]{2,0,1:T(2,128)}), f32[2,32,2560]{2,0,1:T(2,128)S(1)}, u32[]{:S(2)}, u32[]{:S(2)}) async-start(f32[2,32,2560]{2,0,1:T(2,128)} %copy.11), calls=%async_computation.2 | async-start | bytes 1310720 | tf_op jit(solution)/shard_map/all_to_all | solution.py:134
  416.2 22.2 %all-to-all-start.1 = ((f32[8,1,20480]{2,1,0:T(1,128)}), f32[8,1,20480]{2,1,0:T(1,128)S(1)}, u32[]{:S(2)}, u32[]{:S(2)}) async-start(f32[8,1,20480]{2,1,0:T(1,128)} %reshape.190), calls=%async_computation.3 | async-start | bytes 1310720 | tf_op jit(solution)/shard_map/all_to_all | solution.py:142
  448.3 5.0 %copy-start.3 = (f32[1,8,8,40,32]{4,2,3,1,0:T(8,128)S(1)}, f32[1,8,8,40,32]{4,2,3,1,0:T(8,128)}, u32[]{:S(2)}) copy-start(f32[1,8,8,40,32]{4,2,3,1,0:T(8,128)} %get-tuple-element.18) | copy-start | bytes 983044
Sparse Core Ops, SparseCore 0:
  26.5 72.8 all-reduce.2
  110.1 33.5 reduce-scatter.2
  193.5 18.8 all-gather.1
  226.3 70.1 all-reduce.4
  307.2 33.5 reduce-scatter.4
where the time goes:
time: 479 us; the launch traced here: 470 us
  waiting for transfers between devices  256 us (53%)
  blocking collectives  78.9 us (16%)
  matrix products  65.6 us (14%)
  local copies, waits for them, and re-layouts  31.3 us (7%)
  between operations  15.7 us (3%)
  other arithmetic  13.7 us (3%)
  starting transfers between devices  9.51 us (2%)
    psum x2, waiting for transfers between devices, pixel_sum(): return lax.psum(partial_value, 'pix')  143 us
    psum x2, blocking collectives, shards(): gram_total = lax.psum(gram_matrix(applied_share), ('elec', 'pix'))  78.9 us
    reduce_scatter x2, waiting for transfers between devices, shards(): lax.psum_scatter(covariance(waves, projected, mode_count), 'elec', scatte...  67.3 us
    unnamed x18, local copies, waits for them, and re-layouts  19.7 us
    all_gather x1, waiting for transfers between devices, shards(): lax.all_gather(share_low, 'elec', axis=2, tiled=True)  18.5 us
    all_to_all x1, waiting for transfers between devices, shards(): lax.all_to_all(spectrum, 'pix', split_axis=3, concat_axis=2, tiled=True)  16.7 us
    dot_general x2, matrix products, covariance(): lax.dot_general(both, waves, (((0,), (0,)), ((), ())), preferred_element_...  14.1 us
    all_to_all x1, waiting for transfers between devices, shards(): lax.all_to_all(share_modes, 'elec', split_axis=1, concat_axis=2, tiled=True)  9.93 us
  transfers between devices with their start and end apart: 7, of which 7 were waited for; matrix products, arithmetic and copies ran while one was open for 0% of the time, Pallas kernels for 0%

commit v1 on v0

--- a/solution.py
+++ b/solution.py
@@ -103,7 +103,7 @@
 
 
 def pixel_sum(partial_value):
-    return lax.psum(partial_value, "pix")
+    return jnp.sum(lax.all_gather(partial_value, "pix"), axis=0)
 
 
 def shards(wavefronts, trial_modes):

time: 479 us -> 405 us (0.85)
  waiting for transfers between devices: 256 us -> 116 us
  blocking collectives: 78.9 us -> 145 us
  other arithmetic: 13.7 us -> 20.2 us
    psum x2 -> x0, waiting for transfers between devices: 143 us -> none  [pixel_sum(): return lax.psum(partial_value, 'pix')]
    all_gather x0 -> x2, blocking collectives: none -> 66.1 us  [pixel_sum(): return jnp.sum(lax.all_gather(partial_value, 'pix'), axis=0)]
    add x2, other arithmetic: 1.05 us -> 9.16 us  [covariance(): blocks = stacked[:width] + stacked[width:]]
    unnamed x18 -> x26, local copies, waits for them, and re-layouts: 19.7 us -> 17.9 us
  transfers between devices with their start and end apart: 7 -> 5, of which waited for: 7 -> 5; matrix products, arithmetic and copies ran while one was open for 0% -> 0% of each run, Pallas kernels for 0% -> 0%
where the time goes in v1:
time: 405 us; the launch traced here: 398 us
  blocking collectives  145 us (36%)
  waiting for transfers between devices  116 us (29%)
  matrix products  62.7 us (15%)
  local copies, waits for them, and re-layouts  29.2 us (7%)
  other arithmetic  20.2 us (5%)
  between operations  15.5 us (4%)
  starting transfers between devices  9.4 us (2%)
    psum x2, blocking collectives, shards(): gram_total = lax.psum(gram_matrix(applied_share), ('elec', 'pix'))  79.1 us
    reduce_scatter x2, waiting for transfers between devices, shards(): lax.psum_scatter(covariance(waves, projected, mode_count), 'elec', scatte...  70 us
    all_gather x2, blocking collectives, pixel_sum(): return jnp.sum(lax.all_gather(partial_value, 'pix'), axis=0)  66.1 us
    all_gather x1, waiting for transfers between devices, shards(): lax.all_gather(share_low, 'elec', axis=2, tiled=True)  19 us
    unnamed x26, local copies, waits for them, and re-layouts  17.9 us
    all_to_all x1, waiting for transfers between devices, shards(): lax.all_to_all(spectrum, 'pix', split_axis=3, concat_axis=2, tiled=True)  16.7 us
    dot_general x2, matrix products, covariance(): lax.dot_general(both, waves, (((0,), (0,)), ((), ())), preferred_element_...  11.1 us
    all_to_all x1, waiting for transfers between devices, shards(): lax.all_to_all(share_modes, 'elec', split_axis=1, concat_axis=2, tiled=True)  9.93 us
  transfers between devices with their start and end apart: 5, of which 5 were waited for; matrix products, arithmetic and copies ran while one was open for 0% of the time, Pallas kernels for 0%

profile of v1, /device:TPU:0, one launch (start us, length us, event | category | flops | bytes accessed | tf_op | source)
XLA Modules:
  0.0 397.8 jit_solution(4791633833057056039)
XLA Ops:
  6.5 11.1 %copy.19 = bf16[48,8,80,256]{3,1,2,0:T(8,128)(2,1)S(1)} copy(bf16[48,8,80,256]{3,2,1,0:T(8,128)(2,1)} %bitcast.208) | data formatting | bytes 31457280
  23.5 33.8 %all-gather = f32[3072,64]{0,1:T(8,128)S(1)} all-gather(f32[384,64]{0,1:T(8,128)S(1)} %fusion.27), channel_id=2, replica_groups=mesh['elec'=4,'pix'=8] {'pix'}, dimensions={0}, use_global_device_ids=true | all-gather | bytes 884736 | tf_op jit(solution)/shard_map/all_gather | solution.py:106
  57.7 5.6 %fusion.98 = f32[128,20480]{1,0:T(8,128)} fusion(bf16[384,20480]{1,0:T(8,128)(2,1)S(1)} %bitcast.202, bf16[384,64]{0,1:T(8,128)(2,1)S(1)} %get-tuple-element.11, bf16[384,64]{0,1:T(8,128)(2,1)S(1)} %get-tuple-element.12), kind=kOutput, calls=%fused_computation.125 | convolution fusion | flops 2013462528 | bytes 26312704 | tf_op jit(solution)/shard_map/dot_general | solution.py:27
  63.3 4.6 %slice_add_fusion.1 = f32[64,20480]{1,0:T(8,128)S(1)} fusion(f32[128,20480]{1,0:T(8,128)} %fusion.98), kind=kLoop, calls=%fused_computation.9 | loop fusion | flops 1310720 | bytes 15728640 | tf_op jit(solution)/shard_map/add | solution.py:30
  69.9 35.6 %reduce-scatter.3.cloned.1.call-done = f32[2,32,2560]{2,1,0:T(8,128)} async-done(((f32[2,32,10240]{2,1,0:T(8,128)}), f32[2,32,2560]{2,1,0:T(8,128)}) %reduce-scatter.3.cloned.1.call-update) | async-done | bytes 655376 | tf_op jit(solution)/shard_map/reduce_scatter | solution.py:128
  107.4 39.6 %psum.14 = f32[64,64]{1,0:T(8,128)S(1)} all-reduce(f32[64,64]{1,0:T(8,128)S(1)} %fusion.152), channel_id=1, replica_groups=mesh['elec'=4,'pix'=8] {'elec','pix'}, use_global_device_ids=true, to_apply=%region_2.0 | all-reduce | flops 4096 | bytes 32768 | tf_op jit(solution)/shard_map/psum | solution.py:131
  156.6 19.0 %all-gather.4.cloned.1.call-done = bf16[2,32,10240]{2,1,0:T(8,128)(2,1)} async-done(((bf16[2,32,2560]{2,1,0:T(8,128)(2,1)}), bf16[2,32,10240]{2,1,0:T(8,128)(2,1)}) %all-gather.4.cloned.1.call-update) | async-done | bytes 1310736 | tf_op jit(solution)/shard_map/all_gather | solution.py:125
  177.0 5.9 %fusion = f32[64,384]{1,0:T(8,128)S(1)} fusion(bf16[384,20480]{1,0:T(8,128)(2,1)} %bitcast.203, bf16[32,10240]{1,0:T(8,128)(2,1)S(1)} %get-tuple-element.20, bf16[32,10240]{1,0:T(8,128)(2,1)S(1)} %get-tuple-element.19), kind=kOutput, calls=%fused_computation | convolution fusion | flops 505937920 | bytes 9273344 | tf_op jit(solution)/shard_map/dot_general | solution.py:17
  183.0 5.9 %fusion.35 = f32[384,64]{0,1:T(8,128)S(1)} fusion(f32[64,384]{1,0:T(8,128)S(1)} %fusion, bf16[64,10240]{1,0:T(8,128)(2,1)S(1)} %bitcast.222, bf16[384,20480]{1,0:T(8,128)(2,1)} %bitcast.204), kind=kOutput, calls=%fused_computation.38 | convolution fusion | flops 503341056 | bytes 9371648 | tf_op jit(solution)/shard_map/dot_general | solution.py:16
  188.9 32.3 %all-gather.1 = f32[3072,64]{0,1:T(8,128)S(1)} all-gather(f32[384,64]{0,1:T(8,128)S(1)} %fusion.35), channel_id=3, replica_groups=mesh['elec'=4,'pix'=8] {'pix'}, dimensions={0}, use_global_device_ids=true | all-gather | bytes 884736 | tf_op jit(solution)/shard_map/all_gather | solution.py:106
  221.6 5.5 %fusion.102 = f32[128,20480]{1,0:T(8,128)} fusion(bf16[384,20480]{1,0:T(8,128)(2,1)S(1)} %bitcast.207, bf16[384,64]{0,1:T(8,128)(2,1)S(1)} %get-tuple-element.7, bf16[384,64]{0,1:T(8,128)(2,1)S(1)} %get-tuple-element.8), kind=kOutput, calls=%fused_computation.129 | convolution fusion | flops 2013462528 | bytes 26312704 | tf_op jit(solution)/shard_map/dot_general | solution.py:27
  227.1 4.6 %slice_add_fusion = f32[64,20480]{1,0:T(8,128)S(1)} fusion(f32[128,20480]{1,0:T(8,128)} %fusion.102), kind=kLoop, calls=%fused_computation.8 | loop fusion | flops 1310720 | bytes 15728640 | tf_op jit(solution)/shard_map/add | solution.py:30
  233.7 34.4 %reduce-scatter.5.cloned.1.call-done = f32[2,32,2560]{2,1,0:T(8,128)} async-done(((f32[2,32,10240]{2,1,0:T(8,128)}), f32[2,32,2560]{2,1,0:T(8,128)}) %reduce-scatter.5.cloned.1.call-update) | async-done | bytes 655376 | tf_op jit(solution)/shard_map/reduce_scatter | solution.py:128
  270.1 39.4 %psum.15 = f32[64,64]{1,0:T(8,128)S(1)} all-reduce(f32[64,64]{1,0:T(8,128)S(1)} %fusion.165), channel_id=1, replica_groups=mesh['elec'=4,'pix'=8] {'elec','pix'}, use_global_device_ids=true, to_apply=%region_6.7 | all-reduce | flops 4096 | bytes 32768 | tf_op jit(solution)/shard_map/psum | solution.py:131
  318.4 4.0 all-to-all-start
  322.7 9.9 %all-to-all-done = f32[2,32,2560]{2,0,1:T(2,128)S(1)} async-done(((f32[2,32,2560]{2,0,1:T(2,128)}), f32[2,32,2560]{2,0,1:T(2,128)S(1)}, u32[]{:S(2)}, u32[]{:S(2)}) %all-to-all-start) | async-done | bytes 655392 | tf_op jit(solution)/shard_map/all_to_all | solution.py:134
  340.9 2.9 reshape.192
  343.8 5.4 %all-to-all-start.1 = ((f32[8,1,20480]{2,1,0:T(1,128)}), f32[8,1,20480]{2,1,0:T(1,128)S(1)}, u32[]{:S(2)}, u32[]{:S(2)}) async-start(f32[8,1,20480]{2,1,0:T(1,128)} %reshape.192), calls=%async_computation.3 | async-start | bytes 1310720 | tf_op jit(solution)/shard_map/all_to_all | solution.py:142
  349.5 16.7 %all-to-all-done.1 = f32[8,1,20480]{2,1,0:T(1,128)S(1)} async-done(((f32[8,1,20480]{2,1,0:T(1,128)}), f32[8,1,20480]{2,1,0:T(1,128)S(1)}, u32[]{:S(2)}, u32[]{:S(2)}) %all-to-all-start.1) | async-done | bytes 655392 | tf_op jit(solution)/shard_map/all_to_all | solution.py:142
  368.8 3.0 reshape.193
  378.0 2.8 fusion.59
  381.7 2.8 fusion.61
  384.5 2.8 fusion.18
  387.3 2.9 subtract_bitcast_fusion
  (124 shorter events, 51.8 us)
Async XLA Ops:
  6.5 98.9 %reduce-scatter.3.cloned.1.call-start = ((), (), s32[]{:S(2)}) async-start(), calls=%async_computation.4 | async-start | bytes 3276800 | tf_op jit(solution)/shard_map/reduce_scatter | solution.py:128
  6.5 11.1 %copy-start.3 = (f32[2,32,40,256]{3,2,1,0:T(8,128)S(1)}, f32[2,32,40,256]{3,2,1,0:T(8,128)}, u32[]{:S(2)}) copy-start(f32[2,32,40,256]{3,2,1,0:T(8,128)} %param.3) | copy-start | bytes 7864324
  17.7 40.0 %copy-start = (bf16[48,8,80,256]{3,1,2,0:T(8,128)(2,1)}, bf16[48,8,80,256]{3,1,2,0:T(8,128)(2,1)S(1)}, u32[]{:S(2)}) copy-start(bf16[48,8,80,256]{3,1,2,0:T(8,128)(2,1)S(1)} %copy.19) | copy-start | bytes 47185924
  69.9 105.8 %all-gather.4.cloned.1.call-start = ((), (), s32[]{:S(2)}) async-start(), calls=%async_computation.5 | async-start | bytes 1638400 | tf_op jit(solution)/shard_map/all_gather | solution.py:125
  153.9 67.6 %slice-start = ((s8[15728640]{0:T(1024)(128)(4,1)}), s8[3145728]{0:T(1024)(128)(4,1)S(1)}, s32[]{:S(2)}) async-start(s8[15728640]{0:T(1024)(128)(4,1)} %bitcast.205), calls=%async_computation.7 | async-start | bytes 6291456
  156.6 111.5 %reduce-scatter.5.cloned.1.call-start = ((), (), s32[]{:S(2)}) async-start(), calls=%async_computation.6 | async-start | bytes 3276800 | tf_op jit(solution)/shard_map/reduce_scatter | solution.py:128
  177.0 5.9 %copy-start.4 = (bf16[2,32,10240]{2,1,0:T(8,128)(2,1)S(1)}, bf16[2,32,10240]{2,1,0:T(8,128)(2,1)}, u32[]{:S(2)}) copy-start(bf16[2,32,10240]{2,1,0:T(8,128)(2,1)} %all-gather.4.cloned.1.call-done) | copy-start | bytes 3932164
  177.0 44.6 %slice-start.1 = ((s8[15728640]{0:T(1024)(128)(4,1)}), s8[4194304]{0:T(1024)(128)(4,1)S(1)}, s32[]{:S(2)}) async-start(s8[15728640]{0:T(1024)(128)(4,1)} %bitcast.205), calls=%async_computation.8 | async-start | bytes 8388608
  177.0 44.6 %slice-start.2 = ((s8[15728640]{0:T(1024)(128)(4,1)}), s8[4194304]{0:T(1024)(128)(4,1)S(1)}, s32[]{:S(2)}) async-start(s8[15728640]{0:T(1024)(128)(4,1)} %bitcast.205), calls=%async_computation.9 | async-start | bytes 8388608
  183.0 38.6 %slice-start.3 = ((s8[15728640]{0:T(1024)(128)(4,1)}), s8[4194304]{0:T(1024)(128)(4,1)S(1)}, s32[]{:S(2)}) async-start(s8[15728640]{0:T(1024)(128)(4,1)} %bitcast.205), calls=%async_computation.10 | async-start | bytes 8388608
  268.1 48.3 %copy-start.1 = (f32[2,32,2560]{2,1,0:T(8,128)S(1)}, f32[2,32,2560]{2,1,0:T(8,128)}, u32[]{:S(2)}) copy-start(f32[2,32,2560]{2,1,0:T(8,128)} %reduce-scatter.5.cloned.1.call-done) | copy-start | bytes 1966084
  318.4 14.2 %all-to-all-start = ((f32[2,32,2560]{2,0,1:T(2,128)}), f32[2,32,2560]{2,0,1:T(2,128)S(1)}, u32[]{:S(2)}, u32[]{:S(2)}) async-start(f32[2,32,2560]{2,0,1:T(2,128)} %copy.11), calls=%async_computation.2 | async-start | bytes 1310720 | tf_op jit(solution)/shard_map/all_to_all | solution.py:134
  343.8 22.3 %all-to-all-start.1 = ((f32[8,1,20480]{2,1,0:T(1,128)}), f32[8,1,20480]{2,1,0:T(1,128)S(1)}, u32[]{:S(2)}, u32[]{:S(2)}) async-start(f32[8,1,20480]{2,1,0:T(1,128)} %reshape.192), calls=%async_computation.3 | async-start | bytes 1310720 | tf_op jit(solution)/shard_map/all_to_all | solution.py:142
  375.8 5.0 %copy-start.2 = (f32[1,8,8,40,32]{4,2,3,1,0:T(8,128)S(1)}, f32[1,8,8,40,32]{4,2,3,1,0:T(8,128)}, u32[]{:S(2)}) copy-start(f32[1,8,8,40,32]{4,2,3,1,0:T(8,128)} %get-tuple-element.18) | copy-start | bytes 983044
Sparse Core Ops, SparseCore 0:
  70.0 35.4 reduce-scatter.2
  156.7 18.8 all-gather.3
  233.8 34.2 reduce-scatter.4
